TPU v7x, 256 devices: a whole 4x4x8 slice. The times are simulated.
256 devices in a mesh: row: 16 (over z, core), col: 16 (over y, x).
Axes of the slice: x: 4, y: 4, z: 8, core: 2. Of those that a mesh axis runs over, the one named last changes fastest.
Arguments:
- start_basis: float32 [32, 131072], P(None, ('row', 'col')), may hold values from -6 to 6
- degrees: float32 [131072], P(('row', 'col')), may hold values from 0.5 to 1.5
- tiles: float32 [8192, 256, 256], P(('row', 'col')), may hold values from -0.046875 to 0.046875
- tile_rows: int32 [16, 512], P('row', 'col'), may hold values from 0 to 31, as said below
- tile_cols: int32 [16, 512], P('row', 'col'), may hold values from 0 to 31
- counts: int32 [16, 16], P('row', 'col'), may hold values from 1 to 31, as said below
Outputs:
- basis: float32 [32, 131072], P(None, ('row', 'col'))
- projected: float32 [32, 32], replicated
Inputs may be any that keep to these rules, and one draw needn't show every extreme that they name: `tile_rows`: the 32 (row, column) pairs of one device are distinct. counts[r, c] + counts[r', c] <= 32 where r' differs from r by 8; equality holds in column 0.
All inputs are finite; a program needn't handle non-finite values.
Results may differ from a plain program's by a relative error of at most 0.0003.
Values sent between devices are 32-bit elements; how exact they have to be, the bound alone decides.
A program may use at most 64 MiB of HBM per device.

v0:
```python
import jax
import jax.numpy as jnp
from jax import lax
from jax.sharding import PartitionSpec as P

DEGREE = 3


center_shift = 1.0
spread_radius = 1.4
group_width = 8


def tile_products(blocks, tiles, row_local, col_local, live, row_blocks):
    subspace = blocks.shape[0]
    edge = blocks.shape[2]
    block_ids = jnp.arange(row_blocks, dtype=jnp.int32)

    def add_group(index, total):
        start = index * group_width
        group_tiles = lax.dynamic_slice_in_dim(tiles, start, group_width, 0)
        group_rows = lax.dynamic_slice_in_dim(row_local, start, group_width, 0)
        group_cols = lax.dynamic_slice_in_dim(col_local, start, group_width, 0)
        picked = jnp.take(blocks, group_cols, axis=1)
        product = jnp.einsum("kgj,gij->kgi", picked, group_tiles, precision=lax.Precision.HIGHEST)
        valid = start + jnp.arange(group_width, dtype=jnp.int32) < live
        select = ((group_rows[None, :] == block_ids[:, None]) & valid[None, :]).astype(jnp.float32)
        return total + jnp.einsum("ig,kgb->kib", select, product, precision=lax.Precision.HIGHEST)

    initial = jnp.zeros((subspace, row_blocks, edge), jnp.float32)
    return lax.fori_loop(0, (live + group_width - 1) // group_width, add_group, initial)


def inner_products(left, right):
    return jnp.einsum("kn,mn->km", left, right, precision=lax.Precision.HIGHEST)


def body(start_basis, degrees, tiles, tile_rows, tile_cols, counts):
    subspace = start_basis.shape[0]
    edge = tiles.shape[1]
    row_local = tile_rows[0]
    col_local = tile_cols[0]
    live_count = counts[0, 0]
    row_blocks = lax.axis_size("col") * start_basis.shape[1] // edge
    nverts = lax.axis_size("row") * lax.axis_size("col") * start_basis.shape[1]

    def apply_operator(vectors):
        gathered = lax.all_gather(vectors, "row", axis=1, tiled=True)
        blocks = gathered.reshape(subspace, -1, edge)
        partial_value = tile_products(blocks, tiles, row_local, col_local, live_count, row_blocks)
        summed = lax.psum_scatter(
            partial_value.reshape(subspace, -1), "col", scatter_dimension=1, tiled=True
        )
        return degrees[None, :] * vectors - summed

    def shifted(vectors):
        return (apply_operator(vectors) - center_shift * vectors) / spread_radius

    previous = start_basis
    filtered = shifted(start_basis)
    for level in range(DEGREE - 1):
        following = 2.0 * shifted(filtered) - previous
        previous, filtered = (filtered, following)
    gram_matrix = lax.psum(inner_products(filtered, filtered), ("row", "col")) / nverts
    factor = jnp.linalg.cholesky(gram_matrix)
    basis = jax.scipy.linalg.solve_triangular(factor, filtered, lower=True)
    image = apply_operator(basis)
    moment = lax.psum(inner_products(basis, image), ("row", "col")) / nverts
    projected = 0.5 * (moment + moment.T)
    return (basis, projected)


def solution(mesh):
    return jax.shard_map(
        body,
        mesh=mesh,
        in_specs=(
            P(None, ("row", "col")),
            P(("row", "col")),
            P(("row", "col"), None, None),
            P("row", "col"),
            P("row", "col"),
            P("row", "col"),
        ),
        out_specs=(P(None, ("row", "col")), P()),
        check_vma=False,
    )
```

profile of v0, /device:TPU:1, one launch (start us, length us, event | category | flops | bytes accessed | tf_op | source)
XLA Modules:
  0.0 776.6 jit_solution(2379847340742066916)
XLA Ops:
  8.6 44.0 %all-gather.5.cloned.1.call-done = f32[32,8192]{1,0:T(8,128)} async-done(((f32[32,512]{1,0:T(8,128)}), f32[32,8192]{1,0:T(8,128)}) %all-gather.5.cloned.1.call-update) | async-done | bytes 1048592 | tf_op jit(solution)/shard_map/all_gather | solution.py:48
  52.6 1.4 copy.59
  54.1 7.3 while.44
  54.1 1.4 compare_and_fusion.8
  56.1 3.6 fusion.122
  61.4 1.6 copy.40
  63.0 97.4 %reduce-scatter.5.cloned.1.call-done = f32[32,512]{1,0:T(8,128)} async-done(((f32[32,8192]{1,0:T(8,128)}), f32[32,512]{1,0:T(8,128)}) %reduce-scatter.5.cloned.1.call-update) | async-done | bytes 65552 | tf_op jit(solution)/shard_map/reduce_scatter | solution.py:51
  160.4 1.5 fusion.83
  162.0 41.0 %all-gather.7.cloned.1.call-done = f32[32,8192]{1,0:T(8,128)} async-done(((f32[32,512]{1,0:T(8,128)}), f32[32,8192]{1,0:T(8,128)}) %all-gather.7.cloned.1.call-update) | async-done | bytes 1048592 | tf_op jit(solution)/shard_map/all_gather | solution.py:48
  203.0 1.4 copy.58
  204.5 7.3 while.45
  204.5 1.4 compare_and_fusion.9
  206.4 3.6 fusion.128
  211.7 1.6 copy.41
  213.4 97.4 %reduce-scatter.7.cloned.1.call-done = f32[32,512]{1,0:T(8,128)} async-done(((f32[32,8192]{1,0:T(8,128)}), f32[32,512]{1,0:T(8,128)}) %reduce-scatter.7.cloned.1.call-update) | async-done | bytes 65552 | tf_op jit(solution)/shard_map/reduce_scatter | solution.py:51
  310.8 1.5 multiply_subtract_fusion.1
  312.3 40.8 %all-gather.9.cloned.1.call-done = f32[32,8192]{1,0:T(8,128)} async-done(((f32[32,512]{1,0:T(8,128)}), f32[32,8192]{1,0:T(8,128)}) %all-gather.9.cloned.1.call-update) | async-done | bytes 1048592 | tf_op jit(solution)/shard_map/all_gather | solution.py:48
  354.6 7.3 while.46
  354.6 1.4 compare_and_fusion.10
  356.6 3.6 fusion.134
  361.9 1.6 copy.42
  363.5 97.4 %reduce-scatter.9.cloned.1.call-done = f32[32,512]{1,0:T(8,128)} async-done(((f32[32,8192]{1,0:T(8,128)}), f32[32,512]{1,0:T(8,128)}) %reduce-scatter.9.cloned.1.call-update) | async-done | bytes 65552 | tf_op jit(solution)/shard_map/reduce_scatter | solution.py:51
  462.0 77.5 %psum.14 = f32[32,32]{0,1:T(8,128)S(1)} all-reduce(f32[32,32]{0,1:T(8,128)S(1)} %fusion.89), channel_id=1, replica_groups=mesh['row'=16,'col'=16] {'row','col'}, use_global_device_ids=true, to_apply=%region_9.11 | all-reduce | flops 1024 | bytes 8192 | tf_op jit(solution)/shard_map/psum | solution.py:64
  539.6 2.9 cholesky.16
  543.9 2.4 custom-call.7
  547.3 35.6 %all-gather.11.cloned.1.call-done = f32[32,8192]{1,0:T(8,128)} async-done(((f32[32,512]{1,0:T(8,128)}), f32[32,8192]{1,0:T(8,128)}) %all-gather.11.cloned.1.call-update) | async-done | bytes 1048592 | tf_op jit(solution)/shard_map/all_gather | solution.py:48
  584.4 7.3 while.47
  584.5 1.4 compare_and_fusion.11
  586.4 3.6 fusion.140
  591.7 1.6 copy.43
  593.3 97.4 %reduce-scatter.11.cloned.1.call-done = f32[32,512]{1,0:T(8,128)} async-done(((f32[32,8192]{1,0:T(8,128)}), f32[32,512]{1,0:T(8,128)}) %reduce-scatter.11.cloned.1.call-update) | async-done | bytes 65552 | tf_op jit(solution)/shard_map/reduce_scatter | solution.py:51
  691.8 77.3 %psum.15 = f32[32,32]{0,1:T(8,128)S(1)} all-reduce(f32[32,32]{0,1:T(8,128)S(1)} %fusion.80), channel_id=1, replica_groups=mesh['row'=16,'col'=16] {'row','col'}, use_global_device_ids=true, to_apply=%region_15.17 | all-reduce | flops 1024 | bytes 8192 | tf_op jit(solution)/shard_map/psum | solution.py:68
  (64 shorter events, 18.2 us)
Async XLA Ops:
  7.2 45.4 %all-gather.5.cloned.1.call-start = ((), (), s32[]{:S(2)}) async-start(), calls=%async_computation.4 | async-start | bytes 1114112 | tf_op jit(solution)/shard_map/all_gather | solution.py:48
  7.9 152.5 %reduce-scatter.5.cloned.1.call-start = ((), (), s32[]{:S(2)}) async-start(), calls=%async_computation.5 | async-start | bytes 1114112 | tf_op jit(solution)/shard_map/reduce_scatter | solution.py:51
  54.1 106.3 %copy-start = (f32[32,512]{1,0:T(8,128)S(1)}, f32[32,512]{1,0:T(8,128)}, u32[]{:S(2)}) copy-start(f32[32,512]{1,0:T(8,128)} %param.16) | copy-start | bytes 196612
  54.1 106.3 %copy-start.4 = (f32[512]{0:T(512)S(1)}, f32[512]{0:T(512)}, u32[]{:S(2)}) copy-start(f32[512]{0:T(512)} %param.17) | copy-start | bytes 6148
  63.0 140.0 %all-gather.7.cloned.1.call-start = ((), (), s32[]{:S(2)}) async-start(), calls=%async_computation.6 | async-start | bytes 1114112 | tf_op jit(solution)/shard_map/all_gather | solution.py:48
  161.9 148.8 %reduce-scatter.7.cloned.1.call-start = ((), (), s32[]{:S(2)}) async-start(), calls=%async_computation.7 | async-start | bytes 1114112 | tf_op jit(solution)/shard_map/reduce_scatter | solution.py:51
  204.4 106.3 %copy-start.2 = (f32[32,512]{1,0:T(8,128)S(1)}, f32[32,512]{1,0:T(8,128)}, u32[]{:S(2)}) copy-start(f32[32,512]{1,0:T(8,128)} %reduce-scatter.5.cloned.1.call-done) | copy-start | bytes 196612
  213.3 139.8 %all-gather.9.cloned.1.call-start = ((), (), s32[]{:S(2)}) async-start(), calls=%async_computation.8 | async-start | bytes 1114112 | tf_op jit(solution)/shard_map/all_gather | solution.py:48
  312.3 148.6 %reduce-scatter.9.cloned.1.call-start = ((), (), s32[]{:S(2)}) async-start(), calls=%async_computation.9 | async-start | bytes 1114112 | tf_op jit(solution)/shard_map/reduce_scatter | solution.py:51
  354.6 106.3 %copy-start.3 = (f32[32,512]{1,0:T(8,128)S(1)}, f32[32,512]{1,0:T(8,128)}, u32[]{:S(2)}) copy-start(f32[32,512]{1,0:T(8,128)} %multiply_subtract_fusion.1) | copy-start | bytes 196612
  363.5 219.5 %all-gather.11.cloned.1.call-start = ((), (), s32[]{:S(2)}) async-start(), calls=%async_computation.10 | async-start | bytes 1114112 | tf_op jit(solution)/shard_map/all_gather | solution.py:48
  547.3 143.5 %reduce-scatter.11.cloned.1.call-start = ((), (), s32[]{:S(2)}) async-start(), calls=%async_computation.11 | async-start | bytes 1114112 | tf_op jit(solution)/shard_map/reduce_scatter | solution.py:51
  584.4 106.3 %copy-start.1 = (f32[32,512]{1,0:T(8,128)S(1)}, f32[32,512]{1,0:T(8,128)}, u32[]{:S(2)}) copy-start(f32[32,512]{1,0:T(8,128)} %fusion.87) | copy-start | bytes 196612
Sparse Core Ops, SparseCore 0:
  9.8 42.7 all-gather.4
  63.1 97.2 reduce-scatter.4
  162.8 40.0 all-gather.6
  213.5 97.2 reduce-scatter.6
  313.0 40.0 all-gather.8
  363.6 97.2 reduce-scatter.8
  547.4 35.5 all-gather.10
  593.4 97.2 reduce-scatter.10
where the time goes:
time: 778 us; the launch traced here: 777 us
  waiting for transfers between devices  552 us (71%)
  blocking collectives  155 us (20%)
  matrix products  20.2 us (3%)
  local copies, waits for them, and re-layouts  17.6 us (2%)
  other arithmetic  16.7 us (2%)
  between operations  15 us (2%)
    reduce_scatter x4, waiting for transfers between devices, apply_operator(): lax.psum_scatter(partial_value.reshape(subspace, -1), 'col', scatter_dime...  390 us
    all_gather x4, waiting for transfers between devices, apply_operator(): gathered = lax.all_gather(vectors, 'row', axis=1, tiled=True)  161 us
    psum x1, blocking collectives, body(): lax.psum(inner_products(filtered, filtered), ('row', 'col')) / nverts  77.5 us
    psum x1, blocking collectives, body(): moment = lax.psum(inner_products(basis, image), ('row', 'col')) / nverts  77.3 us
  transfers between devices with their start and end apart: 8, of which 8 were waited for; matrix products, arithmetic and copies ran while one was open for 0% of the time, Pallas kernels for 0%

commit v1 on v0

v1 whole, which is shorter than its diff:
```python
import jax
import jax.numpy as jnp
from jax import lax
from jax.experimental import pallas as pl
from jax.experimental.pallas import tpu as pltpu
from jax.sharding import PartitionSpec as P

BS = 256
SUB = 32
TMAX = 32
N_ROW = 16
N_COL = 16
SIDE = 4
Z = 8
NVERT = 131072

CENTER = 1.0
INV_RADIUS = 1.0 / 1.4

F32 = jnp.float32
BF16 = jnp.bfloat16
HIGH = lax.Precision.HIGHEST
NT = (((1,), (1,)), ((), ()))
NN = (((1,), (0,)), ((), ()))


def split(value):
    high = value.astype(BF16)
    return high, (value - high.astype(F32)).astype(BF16)


def pack(square):
    return jnp.concatenate([square[8 * s : 8 * s + 8, :] for s in range(4)], axis=1)


def unpack(flat):
    return jnp.concatenate([flat[:, 32 * s : 32 * s + 32] for s in range(4)], axis=0)


def flip_low(p):
    return p + 1 - 2 * lax.rem(p, 2)


def flip_high(p):
    return lax.rem(p + 3 + 2 * lax.rem(p, 2), SIDE)


def inverse_factor(gram):
    rows = lax.broadcasted_iota(jnp.int32, (32, 128), 0)
    lanes = lax.broadcasted_iota(jnp.int32, (32, 128), 1)
    eye = (rows[:, :32] == lanes[:, :32]).astype(F32)
    table = jnp.concatenate([eye, gram, jnp.zeros((32, 64), F32)], axis=1)
    for j in range(32):
        pivot = table[j : j + 1, 32 + j : 33 + j]
        guess = lax.rsqrt(pivot)
        inv = guess * (1.5 - 0.5 * pivot * guess * guess)
        row = table[j : j + 1, :] * inv
        col = table[:, 32 + j : 33 + j] * inv
        table = jnp.where(rows == j, row, jnp.where(rows > j, table - col * row, table))
    return table[:, :32]


def kernel(index_ref, x_ref, deg_ref, tiles_ref, basis_ref, proj_ref,
           stage, whi, wlo, xg, xs, run, part, land, fcol, fstack, red,
           tile_sem, z_send, z_recv, p_send, p_recv, rs_send, rs_recv,
           fc_send, fc_recv, ar_send, ar_recv):
    r = lax.axis_index("row")
    c = lax.axis_index("col")
    z = r // 2
    core = lax.rem(r, 2)
    cx = lax.rem(c, SIDE)
    cy = c // SIDE

    for t in range(8):
        pltpu.make_async_copy(tiles_ref.at[pl.ds(4 * t, 4)], stage.at[pl.ds(4 * t, 4)], tile_sem.at[t]).start()

    barrier = pltpu.get_barrier_semaphore()
    for q in range(1, 16):
        pl.semaphore_signal(barrier, inc=1, device_id={"row": lax.rem(r + q, 16)})
        pl.semaphore_signal(barrier, inc=1, device_id={"col": lax.rem(c + q, 16)})

    def slot_of(distance):
        return lax.rem(z - distance + Z, Z) * 2 + core

    def z_copy(a, d, hop, h):
        slot = slot_of((hop - 1) * (1 if d == 0 else -1))
        target = lax.rem(z + (1 if d == 0 else Z - 1), Z) * 2 + core
        piece = xg.at[a, slot, h]
        return pltpu.make_async_remote_copy(
            src_ref=piece, dst_ref=piece,
            send_sem=z_send.at[a, d, hop - 1, h], recv_sem=z_recv.at[a, d, hop - 1, h],
            device_id={"row": target})

    def p_copy(a, k, h):
        distance = k if k <= 3 else (4 if k == 7 else 3 - k)
        piece = xg.at[a, slot_of(distance), h]
        return pltpu.make_async_remote_copy(
            src_ref=piece, dst_ref=piece,
            send_sem=p_send.at[a, k, h], recv_sem=p_recv.at[a, k, h],
            device_id={"row": r + 1 - 2 * core})

    def convert(a, slot, h):
        high, low = split(xg[a, slot, h])
        xs[slot * 2 + h, 0:32, :] = high
        xs[slot * 2 + h, 32:64, :] = low

    def exists(d, hop, h):
        return hop <= 3 or (hop == 4 and h == d)

    def gather_start(a):
        for h in range(2):
            for d in range(2):
                z_copy(a, d, 1, h).start()
            p_copy(a, 0, h).start()
        for h in range(2):
            convert(a, r, h)

    def gather_hop(a, hop):
        for h in range(2):
            for d in range(2):
                if exists(d, hop, h):
                    z_copy(a, d, hop, h).wait_recv()
                    if exists(d, hop + 1, h):
                        z_copy(a, d, hop + 1, h).start()
                    k = 7 if hop == 4 else hop + 3 * d
                    p_copy(a, k, h).start()
                    convert(a, slot_of(hop * (1 if d == 0 else -1)), h)

    def gather_end(a):
        for k in range(8):
            distance = k if k <= 3 else (4 if k == 7 else 3 - k)
            slot = slot_of(distance) + 1 - 2 * core
            for h in range(2):
                p_copy(a, k, h).wait_recv()
                convert(a, slot, h)
        for hop in range(1, 5):
            for h in range(2):
                for d in range(2):
                    if exists(d, hop, h):
                        z_copy(a, d, hop, h).wait_send()
        for k in range(8):
            for h in range(2):
                p_copy(a, k, h).wait_send()

    def products():
        def one(t):
            j = index_ref[0, t]
            both = lax.dot_general(xs[j], whi[t], NN, preferred_element_type=F32)
            cross = lax.dot_general(xs[j, 0:32, :], wlo[t], NN, preferred_element_type=F32)
            run[t] = (both[0:32] + both[32:64]) + cross + run[index_ref[1, t]]

        def group(g, carry):
            for u in range(4):
                one(g * 4 + u)
            return carry
        lax.fori_loop(0, TMAX // 4, group, 0)

    def split_tiles(t):
        def one(i, carry):
            high, low = split(stage[i].T)
            whi[i] = high
            wlo[i] = low
            return carry
        lax.fori_loop(4 * t, 4 * t + 4, one, 0)

    flips = (
        {"col": cy * SIDE + flip_low(cx)},
        {"col": cy * SIDE + flip_high(cx)},
        {"col": flip_low(cy) * SIDE + cx},
        {"col": flip_high(cy) * SIDE + cx},
    )

    def owner(bits):
        px, py = cx, cy
        if bits[0]:
            px = flip_low(px)
        if bits[1]:
            px = flip_high(px)
        if bits[2]:
            py = flip_low(py)
        if bits[3]:
            py = flip_high(py)
        return py * SIDE + px

    def place(s, bits):
        return sum(bits[(s + step) % 4] << (3 - step) for step in range(4))

    combos = [tuple((n >> k) & 1 for k in range(4)) for n in range(16)]

    def scatter_copy(a, s, step):
        half = 8 >> step
        start = (0, 8, 12, 14)[step]
        return pltpu.make_async_remote_copy(
            src_ref=part.at[a, s, pl.ds(half, half)],
            dst_ref=land.at[a, s, pl.ds(start, half)],
            send_sem=rs_send.at[a, s, step], recv_sem=rs_recv.at[a, s, step],
            device_id=flips[(s + step) % 4])

    def scatter(a):
        for bits in combos:
            dest = owner(bits)
            for h in range(2):
                block = run[index_ref[2, 2 * dest + h]]
                for s in range(4):
                    part[a, s, place(s, bits), h] = block[8 * s : 8 * s + 8, :]
        for s in range(4):
            scatter_copy(a, s, 0).start()
        for step in range(4):
            half = 8 >> step
            start = (0, 8, 12, 14)[step]
            for s in range(4):
                scatter_copy(a, s, step).wait_recv()
                part[a, s, 0:half] = part[a, s, 0:half] + land[a, s, start : start + half]
                if step < 3:
                    scatter_copy(a, s, step + 1).start()

    def scatter_end(a):
        for s in range(4):
            for step in range(4):
                scatter_copy(a, s, step).wait_send()

    def fcol_copy(s, step):
        size = 1 << step
        return pltpu.make_async_remote_copy(
            src_ref=fcol.at[s, pl.ds(0, size)],
            dst_ref=fcol.at[s, pl.ds(size, size)],
            send_sem=fc_send.at[s, step], recv_sem=fc_recv.at[s, step],
            device_id=flips[(s + 3 - step) % 4])

    def ar_copy(w, level, q):
        if level == 0:
            mine, peer = r, {"row": lax.rem(r + q, 16)}
        else:
            mine, peer = c, {"col": lax.rem(c + q, 16)}
        piece = red.at[w, level, mine]
        return pltpu.make_async_remote_copy(
            src_ref=piece, dst_ref=piece,
            send_sem=ar_send.at[w, level, q], recv_sem=ar_recv.at[w, level, q],
            device_id=peer)

    def ar_start(w, level, value):
        red[w, level, r if level == 0 else c] = value
        for q in range(1, 16):
            ar_copy(w, level, q).start()

    def ar_end(w, level):
        for q in range(1, 16):
            ar_copy(w, level, q).wait_recv()
        total = red[w, level, 0]
        for q in range(1, 16):
            total = total + red[w, level, q]
        for q in range(1, 16):
            ar_copy(w, level, q).wait_send()
        return total

    for h in range(2):
        xg[0, r, h] = x_ref[:, BS * h : BS * h + BS]
    run[TMAX] = jnp.zeros((SUB, BS), F32)
    pl.semaphore_wait(barrier, 30)
    gather_start(0)
    for hop in range(1, 5):
        for t in range(2 * hop - 2, 2 * hop):
            pltpu.make_async_copy(tiles_ref.at[pl.ds(4 * t, 4)], stage.at[pl.ds(4 * t, 4)], tile_sem.at[t]).wait()
            split_tiles(t)
        gather_hop(0, hop)
    gather_end(0)

    for a in range(3):
        if a > 0:
            gather_start(a)
            for hop in range(1, 5):
                gather_hop(a, hop)
            gather_end(a)
        products()
        scatter(a)
        for h in range(2):
            gap = deg_ref[0:1, BS * h : BS * h + BS] - CENTER
            for s in range(4):
                rows = slice(8 * s, 8 * s + 8)
                now = xg[a, r, h, rows, :]
                image = (gap * now - part[a, s, 0, h]) * INV_RADIUS
                if a > 0:
                    image = 2.0 * image - xg[a - 1, r, h, rows, :]
                xg[a + 1, r, h, rows, :] = image
                if a == 2:
                    fcol[s, 0, h] = image
        scatter_end(a)

    gather_start(3)
    for s in range(4):
        fcol_copy(s, 0).start()
    gram = jnp.zeros((SUB, SUB), F32)
    shift = jnp.zeros((SUB, SUB), F32)
    for h in range(2):
        own = xg[3, r, h]
        gram = gram + lax.dot_general(own, own, NT, precision=HIGH, preferred_element_type=F32)
        shift = shift + lax.dot_general(own, own * deg_ref[0:1, BS * h : BS * h + BS], NT, precision=HIGH,
                                        preferred_element_type=F32)
    ar_start(0, 0, pack(gram))

    def column_step(step):
        for s in range(4):
            fcol_copy(s, step).wait_recv()
            if step < 3:
                fcol_copy(s, step + 1).start()

    gather_hop(3, 1)
    column_step(0)
    gather_hop(3, 2)
    column_step(1)
    ar_start(0, 1, ar_end(0, 0))
    gather_hop(3, 3)
    column_step(2)
    gather_hop(3, 4)
    gather_end(3)
    products()
    column_step(3)
    for s in range(4):
        for step in range(4):
            fcol_copy(s, step).wait_send()
    for bits in combos:
        dest = owner(bits)
        for h in range(2):
            for s in range(4):
                piece = fcol[s, place(s, bits), h]
                fstack[2 * dest + h, 8 * s : 8 * s + 8, :] = piece

    def pair(i, acc):
        left = jnp.concatenate(split(fstack[i]), axis=0)
        right = jnp.concatenate(split(run[index_ref[2, i]]), axis=0)
        return acc + lax.dot_general(left, right, NT, preferred_element_type=F32)

    quad = lax.fori_loop(0, 2 * N_COL, pair, jnp.zeros((2 * SUB, 2 * SUB), F32))
    coupling = quad[0:32, 0:32] + quad[0:32, 32:64] + quad[32:64, 0:32] + quad[32:64, 32:64]
    ar_start(1, 0, pack(shift - coupling))
    total_gram = unpack(ar_end(0, 1)) * (1.0 / NVERT)
    inv = inverse_factor(total_gram)
    for h in range(2):
        basis_ref[:, BS * h : BS * h + BS] = lax.dot_general(
            inv, xg[3, r, h], NN, precision=HIGH, preferred_element_type=F32)
    ar_start(1, 1, ar_end(1, 0))
    moment = unpack(ar_end(1, 1)) * (1.0 / NVERT)
    half = lax.dot_general(inv, moment, NN, precision=HIGH, preferred_element_type=F32)
    full = lax.dot_general(half, inv, NT, precision=HIGH, preferred_element_type=F32)
    proj_ref[...] = 0.5 * (full + full.T)


def body(start_basis, degrees, tiles, tile_rows, tile_cols, counts):
    rows = tile_rows[0]
    live = counts[0, 0]
    slot = jnp.arange(TMAX, dtype=jnp.int32)
    earlier = (rows[:, None] == rows[None, :]) & (slot[None, :] < slot[:, None])
    before = jnp.max(jnp.where(earlier, slot[None, :], -1), axis=1)
    before = jnp.where(before < 0, TMAX, before)
    ends = (rows[None, :] == slot[:, None]) & (slot[None, :] < live)
    last = jnp.max(jnp.where(ends, slot[None, :], -1), axis=1)
    last = jnp.where(last < 0, TMAX, last)
    index = jnp.stack([tile_cols[0], before, last])
    vmem = pl.BlockSpec(memory_space=pltpu.VMEM)
    dma = pltpu.SemaphoreType.DMA
    return pl.pallas_call(
        kernel,
        out_shape=(jax.ShapeDtypeStruct((SUB, 2 * BS), F32), jax.ShapeDtypeStruct((SUB, SUB), F32)),
        in_specs=[pl.BlockSpec(memory_space=pltpu.SMEM), vmem, vmem, pl.BlockSpec(memory_space=pl.ANY)],
        out_specs=(vmem, vmem),
        scratch_shapes=[
            pltpu.VMEM((TMAX, BS, BS), F32),
            pltpu.VMEM((TMAX, BS, BS), BF16),
            pltpu.VMEM((TMAX, BS, BS), BF16),
            pltpu.VMEM((4, N_ROW, 2, SUB, BS), F32),
            pltpu.VMEM((2 * N_ROW, 2 * SUB, BS), BF16),
            pltpu.VMEM((TMAX + 1, SUB, BS), F32),
            pltpu.VMEM((3, 4, 16, 2, 8, BS), F32),
            pltpu.VMEM((3, 4, 15, 2, 8, BS), F32),
            pltpu.VMEM((4, 16, 2, 8, BS), F32),
            pltpu.VMEM((2 * N_COL, SUB, BS), F32),
            pltpu.VMEM((2, 2, 16, 8, 128), F32),
            dma((8,)),
            dma((4, 2, 4, 2)), dma((4, 2, 4, 2)),
            dma((4, 8, 2)), dma((4, 8, 2)),
            dma((3, 4, 4)), dma((3, 4, 4)),
            dma((4, 4)), dma((4, 4)),
            dma((2, 2, 16)), dma((2, 2, 16)),
        ],
        compiler_params=pltpu.CompilerParams(collective_id=0, has_side_effects=True, vmem_limit_bytes=56 << 20),
        name="subspace_step",
    )(index, start_basis, degrees.reshape(1, -1), tiles)


def solution(mesh):
    return jax.shard_map(
        body,
        mesh=mesh,
        in_specs=(
            P(None, ("row", "col")),
            P(("row", "col")),
            P(("row", "col"), None, None),
            P("row", "col"),
            P("row", "col"),
            P("row", "col"),
        ),
        out_specs=(P(None, ("row", "col")), P()),
        check_vma=False,
    )
```

time: 778 us -> 154 us (0.20)
  waiting for transfers between devices: 552 us -> 0 us
  blocking collectives: 155 us -> 0 us
  Pallas kernels: 0 us -> 148 us
  matrix products: 20.2 us -> 0 us
  local copies, waits for them, and re-layouts: 17.6 us -> 2.8 us
  other arithmetic: 16.7 us -> 2.17 us
  between operations: 15 us -> 1.3 us
    reduce_scatter x4 -> x0, waiting for transfers between devices: 390 us -> none  [apply_operator(): lax.psum_scatter(partial_value.reshape(subspace, -1), 'col', scatter_dime...]
    all_gather x4 -> x0, waiting for transfers between devices: 161 us -> none  [apply_operator(): gathered = lax.all_gather(vectors, 'row', axis=1, tiled=True)]
    psum x2 -> x0, blocking collectives: 155 us -> none  [the longest x1 77.5 us: body(): lax.psum(inner_products(filtered, filtered), ('row', 'col')) / nverts]
    pallas_call x0 -> x1, Pallas kernels: none -> 148 us  [body(): pl.pallas_call(kernel, out_shape=(jax.ShapeDtypeStruct((SUB, 2 * BS), F32...]
    dot_general x10 -> x0, matrix products: 19.3 us -> none  [the longest x4 14.5 us: add_group(): jnp.einsum('kgj,gij->kgi', picked, group_tiles, precision=lax.Precision.H...]
  transfers between devices with their start and end apart: 8 -> 0, of which waited for: 8 -> 0; matrix products, arithmetic and copies ran while one was open for 0% -> 0% of each run, Pallas kernels for 0% -> 0%
where the time goes in v1:
time: 154 us
  Pallas kernels  148 us (96%)
  local copies, waits for them, and re-layouts  2.8 us (2%)
  other arithmetic  2.17 us (1%)
    pallas_call x1, Pallas kernels, body(): pl.pallas_call(kernel, out_shape=(jax.ShapeDtypeStruct((SUB, 2 * BS), F32...  148 us

profile of v1, /device:TPU:1, one launch (start us, length us, event | category | flops | bytes accessed | tf_op | source)
XLA Modules:
  0.0 154.1 jit_solution(12971943360535398554)
XLA Ops:
  1.3 0.9 select_reduce_fusion.1
  2.2 1.2 pad_add_fusion.index_ref
  3.5 147.9 %subspace_step.1 = (f32[32,512]{1,0:T(8,128)}, f32[32,32]{1,0:T(8,128)}) custom-call(s32[3,32]{1,0:T(4,128)} %pad_add_fusion.index_ref, f32[32,512]{1,0:T(8,128)} %x_ref.1, f32[1,512]{1,0:T(1,128)} %bitcast.9, f32[32,256,256]{2,1,0:T(8,128)} %tiles_ref.1), custom_call_target="tpu_custom_call" | custom-call | tf_op jit(solution)/shard_map/subspace_step/pallas_call | solution.py:361
  151.3 1.5 copy.11
  152.8 1.3 copy.12
  (2 shorter events, 0.0 us)

commit v2 on v1

--- a/solution.py
+++ b/solution.py
@@ -107,13 +107,10 @@
     def exists(d, hop, h):
         return hop <= 3 or (hop == 4 and h == d)
 
-    def gather_start(a):
-        for h in range(2):
-            for d in range(2):
-                z_copy(a, d, 1, h).start()
-            p_copy(a, 0, h).start()
-        for h in range(2):
-            convert(a, r, h)
+    def gather_send(a, h):
+        for d in range(2):
+            z_copy(a, d, 1, h).start()
+        p_copy(a, 0, h).start()
 
     def gather_hop(a, hop):
         for h in range(2):
@@ -187,37 +184,51 @@
 
     combos = [tuple((n >> k) & 1 for k in range(4)) for n in range(16)]
 
-    def scatter_copy(a, s, step):
-        half = 8 >> step
-        start = (0, 8, 12, 14)[step]
+    def pair_bits(s, steps):
+        bits = [0, 0, 0, 0]
+        for step in steps:
+            bits[(s + step) % 4] = 1
+        return tuple(bits)
+
+    def scatter_copy(a, s, h, n):
+        size = (8, 4, 1, 1, 1)[n]
+        first = (8, 4, 2, 1, 3)[n]
+        start = (0, 8, 12, 13, 14)[n]
+        steps = ((0,), (1,), (2,), (3,), (2, 3))[n]
         return pltpu.make_async_remote_copy(
-            src_ref=part.at[a, s, pl.ds(half, half)],
-            dst_ref=land.at[a, s, pl.ds(start, half)],
-            send_sem=rs_send.at[a, s, step], recv_sem=rs_recv.at[a, s, step],
-            device_id=flips[(s + step) % 4])
+            src_ref=part.at[a, s, h, pl.ds(first, size)],
+            dst_ref=land.at[a, s, h, pl.ds(start, size)],
+            send_sem=rs_send.at[a, s, h, n], recv_sem=rs_recv.at[a, s, h, n],
+            device_id={"col": owner(pair_bits(s, steps))})
 
     def scatter(a):
-        for bits in combos:
-            dest = owner(bits)
+        for h in range(2):
+            for bits in combos:
+                block = run[index_ref[2, 2 * owner(bits) + h]]
+                for s in range(4):
+                    part[a, s, h, place(s, bits)] = block[8 * s : 8 * s + 8, :]
+            for s in range(4):
+                scatter_copy(a, s, h, 0).start()
+        for step in range(2):
+            half = 8 >> step
+            start = (0, 8)[step]
             for h in range(2):
-                block = run[index_ref[2, 2 * dest + h]]
                 for s in range(4):
-                    part[a, s, place(s, bits), h] = block[8 * s : 8 * s + 8, :]
-        for s in range(4):
-            scatter_copy(a, s, 0).start()
-        for step in range(4):
-            half = 8 >> step
-            start = (0, 8, 12, 14)[step]
-            for s in range(4):
-                scatter_copy(a, s, step).wait_recv()
-                part[a, s, 0:half] = part[a, s, 0:half] + land[a, s, start : start + half]
-                if step < 3:
-                    scatter_copy(a, s, step + 1).start()
+                    scatter_copy(a, s, h, step).wait_recv()
+                    part[a, s, h, 0:half] = part[a, s, h, 0:half] + land[a, s, h, start : start + half]
+                    for n in ((1,), (4, 2, 3))[step]:
+                        scatter_copy(a, s, h, n).start()
+
+    def scatter_sum(a, s, h):
+        for n in (2, 3, 4):
+            scatter_copy(a, s, h, n).wait_recv()
+        return (part[a, s, h, 0] + land[a, s, h, 12]) + (land[a, s, h, 13] + land[a, s, h, 14])
 
     def scatter_end(a):
         for s in range(4):
-            for step in range(4):
-                scatter_copy(a, s, step).wait_send()
+            for h in range(2):
+                for n in range(5):
+                    scatter_copy(a, s, h, n).wait_send()
 
     def fcol_copy(s, step):
         size = 1 << step
@@ -257,7 +268,10 @@
         xg[0, r, h] = x_ref[:, BS * h : BS * h + BS]
     run[TMAX] = jnp.zeros((SUB, BS), F32)
     pl.semaphore_wait(barrier, 30)
-    gather_start(0)
+    for h in range(2):
+        gather_send(0, h)
+    for h in range(2):
+        convert(0, r, h)
     for hop in range(1, 5):
         for t in range(2 * hop - 2, 2 * hop):
             pltpu.make_async_copy(tiles_ref.at[pl.ds(4 * t, 4)], stage.at[pl.ds(4 * t, 4)], tile_sem.at[t]).wait()
@@ -267,7 +281,6 @@
 
     for a in range(3):
         if a > 0:
-            gather_start(a)
             for hop in range(1, 5):
                 gather_hop(a, hop)
             gather_end(a)
@@ -278,15 +291,17 @@
             for s in range(4):
                 rows = slice(8 * s, 8 * s + 8)
                 now = xg[a, r, h, rows, :]
-                image = (gap * now - part[a, s, 0, h]) * INV_RADIUS
+                image = (gap * now - scatter_sum(a, s, h)) * INV_RADIUS
                 if a > 0:
                     image = 2.0 * image - xg[a - 1, r, h, rows, :]
                 xg[a + 1, r, h, rows, :] = image
                 if a == 2:
                     fcol[s, 0, h] = image
+            gather_send(a + 1, h)
+        for h in range(2):
+            convert(a + 1, r, h)
         scatter_end(a)
 
-    gather_start(3)
     for s in range(4):
         fcol_copy(s, 0).start()
     gram = jnp.zeros((SUB, SUB), F32)
@@ -325,12 +340,15 @@
                 piece = fcol[s, place(s, bits), h]
                 fstack[2 * dest + h, 8 * s : 8 * s + 8, :] = piece
 
-    def pair(i, acc):
+    def pair(i):
         left = jnp.concatenate(split(fstack[i]), axis=0)
         right = jnp.concatenate(split(run[index_ref[2, i]]), axis=0)
-        return acc + lax.dot_general(left, right, NT, preferred_element_type=F32)
-
-    quad = lax.fori_loop(0, 2 * N_COL, pair, jnp.zeros((2 * SUB, 2 * SUB), F32))
+        return lax.dot_general(left, right, NT, preferred_element_type=F32)
+
+    def pairs(g, acc):
+        return acc + ((pair(4 * g) + pair(4 * g + 1)) + (pair(4 * g + 2) + pair(4 * g + 3)))
+
+    quad = lax.fori_loop(0, N_COL // 2, pairs, jnp.zeros((2 * SUB, 2 * SUB), F32))
     coupling = quad[0:32, 0:32] + quad[0:32, 32:64] + quad[32:64, 0:32] + quad[32:64, 32:64]
     ar_start(1, 0, pack(shift - coupling))
     total_gram = unpack(ar_end(0, 1)) * (1.0 / NVERT)
@@ -370,15 +388,15 @@
             pltpu.VMEM((4, N_ROW, 2, SUB, BS), F32),
             pltpu.VMEM((2 * N_ROW, 2 * SUB, BS), BF16),
             pltpu.VMEM((TMAX + 1, SUB, BS), F32),
-            pltpu.VMEM((3, 4, 16, 2, 8, BS), F32),
-            pltpu.VMEM((3, 4, 15, 2, 8, BS), F32),
+            pltpu.VMEM((3, 4, 2, 16, 8, BS), F32),
+            pltpu.VMEM((3, 4, 2, 15, 8, BS), F32),
             pltpu.VMEM((4, 16, 2, 8, BS), F32),
             pltpu.VMEM((2 * N_COL, SUB, BS), F32),
             pltpu.VMEM((2, 2, 16, 8, 128), F32),
             dma((8,)),
             dma((4, 2, 4, 2)), dma((4, 2, 4, 2)),
             dma((4, 8, 2)), dma((4, 8, 2)),
-            dma((3, 4, 4)), dma((3, 4, 4)),
+            dma((3, 4, 2, 5)), dma((3, 4, 2, 5)),
             dma((4, 4)), dma((4, 4)),
             dma((2, 2, 16)), dma((2, 2, 16)),
         ],

time: 154 us -> 141 us (0.916)
  Pallas kernels: 148 us -> 135 us
    pallas_call x1, Pallas kernels: 148 us -> 135 us  [body(): pl.pallas_call(kernel, out_shape=(jax.ShapeDtypeStruct((SUB, 2 * BS), F32...]
where the time goes in v2:
time: 141 us
  Pallas kernels  135 us (96%)
  local copies, waits for them, and re-layouts  2.8 us (2%)
  other arithmetic  2.17 us (2%)
    pallas_call x1, Pallas kernels, body(): pl.pallas_call(kernel, out_shape=(jax.ShapeDtypeStruct((SUB, 2 * BS), F32...  135 us

profile of v2, /device:TPU:1, one launch (start us, length us, event | category | flops | bytes accessed | tf_op | source)
XLA Modules:
  0.0 140.8 jit_solution(15343932967340691752)
XLA Ops:
  1.3 0.9 select_reduce_fusion.1
  2.2 1.2 pad_add_fusion.index_ref
  3.5 134.5 %subspace_step.1 = (f32[32,512]{1,0:T(8,128)}, f32[32,32]{1,0:T(8,128)}) custom-call(s32[3,32]{1,0:T(4,128)} %pad_add_fusion.index_ref, f32[32,512]{1,0:T(8,128)} %x_ref.1, f32[1,512]{1,0:T(1,128)} %bitcast.9, f32[32,256,256]{2,1,0:T(8,128)} %tiles_ref.1), custom_call_target="tpu_custom_call" | custom-call | tf_op jit(solution)/shard_map/subspace_step/pallas_call | solution.py:379
  138.0 1.5 %copy.11 = f32[32,512]{1,0:T(8,128)} copy(f32[32,512]{1,0:T(8,128)} %get-tuple-element.8) | data formatting | bytes 131072
  139.5 1.3 copy.12
  (2 shorter events, 0.0 us)

commit v3 on v2

--- a/solution.py
+++ b/solution.py
@@ -61,7 +61,7 @@
 
 
 def kernel(index_ref, x_ref, deg_ref, tiles_ref, basis_ref, proj_ref,
-           stage, whi, wlo, xg, xs, run, part, land, fcol, fstack, red,
+           stage, whi, wlo, xg, xs, run, part, land, fcol, red,
            tile_sem, z_send, z_recv, p_send, p_recv, rs_send, rs_recv,
            fc_send, fc_recv, ar_send, ar_recv):
     r = lax.axis_index("row")
@@ -82,13 +82,13 @@
     def slot_of(distance):
         return lax.rem(z - distance + Z, Z) * 2 + core
 
-    def z_copy(a, d, hop, h):
+    def z_copy(a, d, hop, q):
         slot = slot_of((hop - 1) * (1 if d == 0 else -1))
         target = lax.rem(z + (1 if d == 0 else Z - 1), Z) * 2 + core
-        piece = xg.at[a, slot, h]
+        piece = xg.at[a, slot, q // 2, pl.ds(16 * (q % 2), 16)]
         return pltpu.make_async_remote_copy(
             src_ref=piece, dst_ref=piece,
-            send_sem=z_send.at[a, d, hop - 1, h], recv_sem=z_recv.at[a, d, hop - 1, h],
+            send_sem=z_send.at[a, d, hop - 1, q], recv_sem=z_recv.at[a, d, hop - 1, q],
             device_id={"row": target})
 
     def p_copy(a, k, h):
@@ -108,20 +108,23 @@
         return hop <= 3 or (hop == 4 and h == d)
 
     def gather_send(a, h):
-        for d in range(2):
-            z_copy(a, d, 1, h).start()
+        for q in (2 * h, 2 * h + 1):
+            for d in range(2):
+                z_copy(a, d, 1, q).start()
         p_copy(a, 0, h).start()
 
     def gather_hop(a, hop):
-        for h in range(2):
+        for q in range(4):
+            h = q // 2
             for d in range(2):
                 if exists(d, hop, h):
-                    z_copy(a, d, hop, h).wait_recv()
+                    z_copy(a, d, hop, q).wait_recv()
                     if exists(d, hop + 1, h):
-                        z_copy(a, d, hop + 1, h).start()
-                    k = 7 if hop == 4 else hop + 3 * d
-                    p_copy(a, k, h).start()
-                    convert(a, slot_of(hop * (1 if d == 0 else -1)), h)
+                        z_copy(a, d, hop + 1, q).start()
+                    if q % 2 == 1:
+                        k = 7 if hop == 4 else hop + 3 * d
+                        p_copy(a, k, h).start()
+                        convert(a, slot_of(hop * (1 if d == 0 else -1)), h)
 
     def gather_end(a):
         for k in range(8):
@@ -131,10 +134,10 @@
                 p_copy(a, k, h).wait_recv()
                 convert(a, slot, h)
         for hop in range(1, 5):
-            for h in range(2):
+            for q in range(4):
                 for d in range(2):
-                    if exists(d, hop, h):
-                        z_copy(a, d, hop, h).wait_send()
+                    if exists(d, hop, q // 2):
+                        z_copy(a, d, hop, q).wait_send()
         for k in range(8):
             for h in range(2):
                 p_copy(a, k, h).wait_send()
@@ -201,28 +204,38 @@
             send_sem=rs_send.at[a, s, h, n], recv_sem=rs_recv.at[a, s, h, n],
             device_id={"col": owner(pair_bits(s, steps))})
 
+    def scatter_place(a, h, sent):
+        for bits in combos:
+            block = run[index_ref[2, 2 * owner(bits) + h]]
+            for s in range(4):
+                if bits[s] == sent:
+                    part[a, s, h, place(s, bits)] = block[8 * s : 8 * s + 8, :]
+
     def scatter(a):
         for h in range(2):
-            for bits in combos:
-                block = run[index_ref[2, 2 * owner(bits) + h]]
-                for s in range(4):
-                    part[a, s, h, place(s, bits)] = block[8 * s : 8 * s + 8, :]
+            scatter_place(a, h, 1)
             for s in range(4):
                 scatter_copy(a, s, h, 0).start()
-        for step in range(2):
-            half = 8 >> step
-            start = (0, 8)[step]
-            for h in range(2):
-                for s in range(4):
-                    scatter_copy(a, s, h, step).wait_recv()
-                    part[a, s, h, 0:half] = part[a, s, h, 0:half] + land[a, s, h, start : start + half]
-                    for n in ((1,), (4, 2, 3))[step]:
-                        scatter_copy(a, s, h, n).start()
+        for h in range(2):
+            scatter_place(a, h, 0)
+        for h in range(2):
+            for s in range(4):
+                scatter_copy(a, s, h, 0).wait_recv()
+                part[a, s, h, 4:8] = part[a, s, h, 4:8] + land[a, s, h, 4:8]
+                scatter_copy(a, s, h, 1).start()
+                part[a, s, h, 0:4] = part[a, s, h, 0:4] + land[a, s, h, 0:4]
+        for h in range(2):
+            for s in range(4):
+                scatter_copy(a, s, h, 1).wait_recv()
+                part[a, s, h, 1:4] = part[a, s, h, 1:4] + land[a, s, h, 9:12]
+                for n in (4, 2, 3):
+                    scatter_copy(a, s, h, n).start()
 
     def scatter_sum(a, s, h):
         for n in (2, 3, 4):
             scatter_copy(a, s, h, n).wait_recv()
-        return (part[a, s, h, 0] + land[a, s, h, 12]) + (land[a, s, h, 13] + land[a, s, h, 14])
+        own = part[a, s, h, 0] + land[a, s, h, 8]
+        return (own + land[a, s, h, 12]) + (land[a, s, h, 13] + land[a, s, h, 14])
 
     def scatter_end(a):
         for s in range(4):
@@ -333,22 +346,13 @@
     for s in range(4):
         for step in range(4):
             fcol_copy(s, step).wait_send()
+    quad = jnp.zeros((2 * SUB, 2 * SUB), F32)
     for bits in combos:
-        dest = owner(bits)
-        for h in range(2):
-            for s in range(4):
-                piece = fcol[s, place(s, bits), h]
-                fstack[2 * dest + h, 8 * s : 8 * s + 8, :] = piece
-
-    def pair(i):
-        left = jnp.concatenate(split(fstack[i]), axis=0)
-        right = jnp.concatenate(split(run[index_ref[2, i]]), axis=0)
-        return lax.dot_general(left, right, NT, preferred_element_type=F32)
-
-    def pairs(g, acc):
-        return acc + ((pair(4 * g) + pair(4 * g + 1)) + (pair(4 * g + 2) + pair(4 * g + 3)))
-
-    quad = lax.fori_loop(0, N_COL // 2, pairs, jnp.zeros((2 * SUB, 2 * SUB), F32))
+        for h in range(2):
+            mine = jnp.concatenate([fcol[s, place(s, bits), h] for s in range(4)], axis=0)
+            left = jnp.concatenate(split(mine), axis=0)
+            right = jnp.concatenate(split(run[index_ref[2, 2 * owner(bits) + h]]), axis=0)
+            quad = quad + lax.dot_general(left, right, NT, preferred_element_type=F32)
     coupling = quad[0:32, 0:32] + quad[0:32, 32:64] + quad[32:64, 0:32] + quad[32:64, 32:64]
     ar_start(1, 0, pack(shift - coupling))
     total_gram = unpack(ar_end(0, 1)) * (1.0 / NVERT)
@@ -391,10 +395,9 @@
             pltpu.VMEM((3, 4, 2, 16, 8, BS), F32),
             pltpu.VMEM((3, 4, 2, 15, 8, BS), F32),
             pltpu.VMEM((4, 16, 2, 8, BS), F32),
-            pltpu.VMEM((2 * N_COL, SUB, BS), F32),
             pltpu.VMEM((2, 2, 16, 8, 128), F32),
             dma((8,)),
-            dma((4, 2, 4, 2)), dma((4, 2, 4, 2)),
+            dma((4, 2, 4, 4)), dma((4, 2, 4, 4)),
             dma((4, 8, 2)), dma((4, 8, 2)),
             dma((3, 4, 2, 5)), dma((3, 4, 2, 5)),
             dma((4, 4)), dma((4, 4)),

time: 141 us -> 142 us (level)
  no operation moved by 1% of the time
where the time goes in v3:
time: 142 us
  Pallas kernels  136 us (96%)
  local copies, waits for them, and re-layouts  2.8 us (2%)
  other arithmetic  2.17 us (2%)
    pallas_call x1, Pallas kernels, body(): pl.pallas_call(kernel, out_shape=(jax.ShapeDtypeStruct((SUB, 2 * BS), F32...  136 us

profile of v3, /device:TPU:1, one launch (start us, length us, event | category | flops | bytes accessed | tf_op | source)
XLA Modules:
  0.0 141.9 jit_solution(11541153806194524440)
XLA Ops:
  1.3 0.9 select_reduce_fusion.1
  2.2 1.2 pad_add_fusion.index_ref
  3.5 135.6 %subspace_step.1 = (f32[32,512]{1,0:T(8,128)}, f32[32,32]{1,0:T(8,128)}) custom-call(s32[3,32]{1,0:T(4,128)} %pad_add_fusion.index_ref, f32[32,512]{1,0:T(8,128)} %x_ref.1, f32[1,512]{1,0:T(1,128)} %bitcast.9, f32[32,256,256]{2,1,0:T(8,128)} %tiles_ref.1), custom_call_target="tpu_custom_call" | custom-call | tf_op jit(solution)/shard_map/subspace_step/pallas_call | solution.py:383
  139.1 1.5 %copy.11 = f32[32,512]{1,0:T(8,128)} copy(f32[32,512]{1,0:T(8,128)} %get-tuple-element.8) | data formatting | bytes 131072
  140.6 1.3 copy.12
  (2 shorter events, 0.0 us)

commit v4 on v3

--- a/solution.py
+++ b/solution.py
@@ -82,13 +82,13 @@
     def slot_of(distance):
         return lax.rem(z - distance + Z, Z) * 2 + core
 
-    def z_copy(a, d, hop, q):
+    def z_copy(a, d, hop, h):
         slot = slot_of((hop - 1) * (1 if d == 0 else -1))
         target = lax.rem(z + (1 if d == 0 else Z - 1), Z) * 2 + core
-        piece = xg.at[a, slot, q // 2, pl.ds(16 * (q % 2), 16)]
+        piece = xg.at[a, slot, h]
         return pltpu.make_async_remote_copy(
             src_ref=piece, dst_ref=piece,
-            send_sem=z_send.at[a, d, hop - 1, q], recv_sem=z_recv.at[a, d, hop - 1, q],
+            send_sem=z_send.at[a, d, hop - 1, h], recv_sem=z_recv.at[a, d, hop - 1, h],
             device_id={"row": target})
 
     def p_copy(a, k, h):
@@ -108,23 +108,20 @@
         return hop <= 3 or (hop == 4 and h == d)
 
     def gather_send(a, h):
-        for q in (2 * h, 2 * h + 1):
-            for d in range(2):
-                z_copy(a, d, 1, q).start()
+        for d in range(2):
+            z_copy(a, d, 1, h).start()
         p_copy(a, 0, h).start()
 
     def gather_hop(a, hop):
-        for q in range(4):
-            h = q // 2
+        for h in range(2):
             for d in range(2):
                 if exists(d, hop, h):
-                    z_copy(a, d, hop, q).wait_recv()
+                    z_copy(a, d, hop, h).wait_recv()
                     if exists(d, hop + 1, h):
-                        z_copy(a, d, hop + 1, q).start()
-                    if q % 2 == 1:
-                        k = 7 if hop == 4 else hop + 3 * d
-                        p_copy(a, k, h).start()
-                        convert(a, slot_of(hop * (1 if d == 0 else -1)), h)
+                        z_copy(a, d, hop + 1, h).start()
+                    k = 7 if hop == 4 else hop + 3 * d
+                    p_copy(a, k, h).start()
+                    convert(a, slot_of(hop * (1 if d == 0 else -1)), h)
 
     def gather_end(a):
         for k in range(8):
@@ -134,10 +131,10 @@
                 p_copy(a, k, h).wait_recv()
                 convert(a, slot, h)
         for hop in range(1, 5):
-            for q in range(4):
+            for h in range(2):
                 for d in range(2):
-                    if exists(d, hop, q // 2):
-                        z_copy(a, d, hop, q).wait_send()
+                    if exists(d, hop, h):
+                        z_copy(a, d, hop, h).wait_send()
         for k in range(8):
             for h in range(2):
                 p_copy(a, k, h).wait_send()
@@ -397,7 +394,7 @@
             pltpu.VMEM((4, 16, 2, 8, BS), F32),
             pltpu.VMEM((2, 2, 16, 8, 128), F32),
             dma((8,)),
-            dma((4, 2, 4, 4)), dma((4, 2, 4, 4)),
+            dma((4, 2, 4, 2)), dma((4, 2, 4, 2)),
             dma((4, 8, 2)), dma((4, 8, 2)),
             dma((3, 4, 2, 5)), dma((3, 4, 2, 5)),
             dma((4, 4)), dma((4, 4)),

time: 142 us -> 140 us (0.986)
  Pallas kernels: 136 us -> 133 us
    pallas_call x1, Pallas kernels: 136 us -> 133 us  [body(): pl.pallas_call(kernel, out_shape=(jax.ShapeDtypeStruct((SUB, 2 * BS), F32...]
where the time goes in v4:
time: 140 us
  Pallas kernels  133 us (95%)
  local copies, waits for them, and re-layouts  2.8 us (2%)
  other arithmetic  2.17 us (2%)
    pallas_call x1, Pallas kernels, body(): pl.pallas_call(kernel, out_shape=(jax.ShapeDtypeStruct((SUB, 2 * BS), F32...  133 us

profile of v4, /device:TPU:1, one launch (start us, length us, event | category | flops | bytes accessed | tf_op | source)
XLA Modules:
  0.0 139.8 jit_solution(7921224643985075632)
XLA Ops:
  1.3 0.9 select_reduce_fusion.1
  2.2 1.2 pad_add_fusion.index_ref
  3.5 133.5 %subspace_step.1 = (f32[32,512]{1,0:T(8,128)}, f32[32,32]{1,0:T(8,128)}) custom-call(s32[3,32]{1,0:T(4,128)} %pad_add_fusion.index_ref, f32[32,512]{1,0:T(8,128)} %x_ref.1, f32[1,512]{1,0:T(1,128)} %bitcast.9, f32[32,256,256]{2,1,0:T(8,128)} %tiles_ref.1), custom_call_target="tpu_custom_call" | custom-call | tf_op jit(solution)/shard_map/subspace_step/pallas_call | solution.py:380
  137.0 1.5 %copy.11 = f32[32,512]{1,0:T(8,128)} copy(f32[32,512]{1,0:T(8,128)} %get-tuple-element.8) | data formatting | bytes 131072
  138.4 1.3 copy.12
  (2 shorter events, 0.0 us)
